TPU v7x, 32 devices: a whole 2x2x4 slice. The times are simulated.
32 devices in a mesh: group: 2 (over y), tm: 4 (over x, core), space: 4 (over z).
Axes of the slice: x: 2, y: 2, z: 4, core: 2. Of those that a mesh axis runs over, the one named last changes fastest.
Arguments:
- latent: bfloat16 [8, 16, 4, 128], P(('group', 'tm'), None, 'space'), parts along dimension 0, may hold values from -27 to 27
- conv_weight: bfloat16 [3, 3, 3, 16, 512], replicated, may hold values from -0.3125 to 0.3125
- norm_gain: float32 [512], replicated, may hold values from 0.25 to 1.75
- qkv_weight: bfloat16 [512, 1536], replicated, may hold values from -0.25 to 0.25
- out_weight: bfloat16 [512, 512], replicated, may hold values from -0.25 to 0.25
- grad_out: bfloat16 [8, 4, 128, 512], P(('group', 'tm'), 'space'), parts along dimension 0, may hold values from -6 to 6
Outputs:
- grad_latent: float32 [8, 16, 4, 128], P(('group', 'tm'), None, 'space'), parts along dimension 0
There are 2 independent parts, one for each index of `group`. A program takes and returns all parts, laid end to end along the dimension named above; an argument that names none is the same for every part. Nothing has to cross between parts.
All inputs are finite; a program needn't handle non-finite values.
Results may differ from a plain program's by a relative error of at most 0.013.
The roundings to bfloat16 on the way count: a program that leaves them out, or rounds other values in their place, can miss the bound.
Values may be sent and summed in bfloat16 or wider, within the bound.
A program may use at most 64 MiB of HBM per device.

v0:
```python
import jax
import jax.numpy as jnp
from jax import lax
from jax.sharding import PartitionSpec as P

GROUPS = 32
EPSILON = 1e-06


def from_behind(value, axis, steps):
    count = lax.axis_size(axis)
    leading, last = (max(0, -steps), min(count, count - steps))
    return lax.ppermute(value, axis, [(source, source + steps) for source in range(leading, last)])


def padded_2(value, sides, width):
    for axis, dim in sides:
        count, length = (lax.axis_size(axis), value.shape[dim])
        up = [(i, (i + 1) % count) for i in range(count - 1)]
        down = [(j, i) for i, j in up]
        last = lax.slice_in_dim(value, length - width, length, axis=dim)
        leading = lax.slice_in_dim(value, 0, width, axis=dim)
        before = lax.ppermute(last, axis, up)
        after = lax.ppermute(leading, axis, down)
        value = jnp.concatenate([before, value, after], axis=dim)
    return value


def contract(left, right, left_dim, right_dim):
    return lax.dot_general(
        left, right, (((left_dim,), (right_dim,)), ((), ())), preferred_element_type=jnp.float32
    )


def on_device(latent, conv_weight, norm_gain, qkv_weight, out_weight, grad_out):
    lat_width = latent.shape[1]
    row_count = latent.shape[2]
    col_count = latent.shape[3]
    channels = grad_out.shape[3]
    cells = row_count * col_count
    per_group = channels // GROUPS
    scaling = channels ** (-0.5)
    conv_flat = conv_weight.reshape(27 * lat_width, channels)
    far_frame = from_behind(latent, "tm", 2)
    near_frame = from_behind(latent, "tm", 1)
    window = jnp.concatenate([far_frame, near_frame, latent], axis=0)
    haloed = padded_2(window, (("space", 2),), 1)
    padded = jnp.pad(haloed, ((0, 0), (0, 0), (0, 0), (1, 1)))
    pieces = []
    for a in range(3):
        for b in range(3):
            for e in range(3):
                pieces.append(padded[2 - a, :, b : b + row_count, e : e + col_count])
    patches = jnp.concatenate(pieces, axis=0).reshape(27 * lat_width, cells)
    hidden = contract(patches, conv_flat, 0, 0)
    grouped = hidden.reshape(cells, GROUPS, per_group)
    count_all = float(lax.axis_size("space") * cells * per_group)
    sum_plain, sum_square = lax.psum(
        (jnp.sum(grouped, axis=(0, 2)), jnp.sum(grouped * grouped, axis=(0, 2))), "space"
    )
    average = sum_plain / count_all
    spread = sum_square / count_all - average * average
    inverse = lax.rsqrt(spread + EPSILON)
    unit_cells = (grouped - average[None, :, None]) * inverse[None, :, None]
    gain_grid = norm_gain.reshape(GROUPS, per_group)
    normed = (unit_cells * gain_grid).astype(jnp.bfloat16).reshape(cells, channels)
    projected = jnp.dot(normed, qkv_weight, preferred_element_type=jnp.float32).astype(jnp.bfloat16)
    query_part = projected[:, :channels]
    key_part = projected[:, channels : 2 * channels]
    value_part = projected[:, 2 * channels :]
    upstream = grad_out.reshape(cells, channels)
    grad_att = contract(upstream, out_weight, 1, 1).astype(jnp.bfloat16)
    largest = jnp.full((cells,), -1e30, jnp.float32)
    scores = (
        contract(query_part, lax.all_gather(key_part, "space", axis=0, tiled=True), 1, 1) * scaling
    )
    highest = jnp.maximum(largest, jnp.max(scores, axis=1))
    running = jnp.sum(jnp.exp(scores - highest[:, None]), axis=1)
    largest, running = (highest, running)
    log_norm = largest + jnp.log(running)
    key_piece = lax.all_gather(key_part, "space", axis=0, tiled=True)
    value_piece = lax.all_gather(value_part, "space", axis=0, tiled=True)
    scores = contract(query_part, key_piece, 1, 1) * scaling
    soft_bf = jnp.exp(scores - log_norm[:, None]).astype(jnp.bfloat16)
    attended = jnp.dot(soft_bf, value_piece, preferred_element_type=jnp.float32)
    attended = lax.optimization_barrier(attended.astype(jnp.bfloat16))
    row_delta = jnp.sum(grad_att.astype(jnp.float32) * attended.astype(jnp.float32), axis=1)
    key_piece = lax.all_gather(key_part, "space", axis=0, tiled=True)
    value_piece = lax.all_gather(value_part, "space", axis=0, tiled=True)
    scores = contract(query_part, key_piece, 1, 1) * scaling
    soft_probs = jnp.exp(scores - log_norm[:, None])
    grad_probs = contract(grad_att, value_piece, 1, 1)
    dscore = (soft_probs * (grad_probs - row_delta[:, None]) * scaling).astype(jnp.bfloat16)
    grad_query = jnp.dot(dscore, key_piece, preferred_element_type=jnp.float32).astype(jnp.bfloat16)
    all_norms, all_deltas = (
        lax.all_gather(log_norm, "space", axis=0, tiled=True),
        lax.all_gather(row_delta, "space", axis=0, tiled=True),
    )
    query_piece = lax.all_gather(query_part, "space", axis=0, tiled=True)
    grad_piece = lax.all_gather(grad_att, "space", axis=0, tiled=True)
    scores = contract(query_piece, key_part, 1, 1) * scaling
    soft_probs = jnp.exp(scores - all_norms[:, None])
    soft_bf = soft_probs.astype(jnp.bfloat16)
    grad_probs = contract(grad_piece, value_part, 1, 1)
    dscore = (soft_probs * (grad_probs - all_deltas[:, None]) * scaling).astype(jnp.bfloat16)
    key_accum = contract(dscore, query_piece, 0, 0)
    value_accum = contract(soft_bf, grad_piece, 0, 0)
    grad_proj = jnp.concatenate(
        [grad_query, key_accum.astype(jnp.bfloat16), value_accum.astype(jnp.bfloat16)], axis=1
    )
    grad_normed = contract(grad_proj, qkv_weight, 1, 1)
    scaled = grad_normed.reshape(cells, GROUPS, per_group) * gain_grid
    grad_first, grad_second = lax.psum(
        (jnp.sum(scaled, axis=(0, 2)), jnp.sum(scaled * unit_cells, axis=(0, 2))), "space"
    )
    first_mean = grad_first / count_all
    second_mean = grad_second / count_all
    grad_hidden = upstream.astype(jnp.float32).reshape(cells, GROUPS, per_group)
    grad_hidden = (
        grad_hidden
        + (scaled - first_mean[None, :, None] - unit_cells * second_mean[None, :, None])
        * inverse[None, :, None]
    )
    grad_hidden = grad_hidden.astype(jnp.bfloat16).reshape(1, row_count, col_count, channels)
    after_one = from_behind(grad_hidden, "tm", -1)
    after_two = from_behind(grad_hidden, "tm", -2)
    window_grad = jnp.concatenate([grad_hidden, after_one, after_two], axis=0)
    haloed_grad = padded_2(window_grad, (("space", 1),), 1)
    summed = jnp.zeros((lat_width, row_count, col_count), jnp.float32)
    tap_rows = 9 * lat_width
    for a in range(3):
        columns = contract(
            conv_flat[a * tap_rows : (a + 1) * tap_rows], haloed_grad[a].reshape(-1, channels), 1, 1
        )
        columns = columns.reshape(3, 3, lat_width, row_count + 2, col_count)
        columns = jnp.pad(columns, ((0, 0), (0, 0), (0, 0), (0, 0), (1, 1)))
        for b in range(3):
            for e in range(3):
                summed = (
                    summed + columns[b, e, :, 2 - b : 2 - b + row_count, 2 - e : 2 - e + col_count]
                )
    return summed[None]


def solution(mesh):
    return jax.shard_map(
        on_device,
        mesh=mesh,
        in_specs=(
            P(("group", "tm"), None, "space", None),
            P(),
            P(),
            P(),
            P(),
            P(("group", "tm"), "space", None, None),
        ),
        out_specs=P(("group", "tm"), None, "space", None),
        check_vma=False,
    )
```

profile of v0, /device:TPU:0, one launch (start us, length us, event | category | flops | bytes accessed | tf_op | source)
XLA Modules:
  0.0 157.7 jit_solution(4442520707237397019)
XLA Ops:
  0.0 5.0 %collective-permute-start = (bf16[1,16,1,128]{3,1,2,0:T(8,128)(2,1)}, bf16[1,16,1,128]{3,1,2,0:T(8,128)(2,1)S(1)}, u32[]{:S(2)}, u32[]{:S(2)}) collective-permute-start(bf16[1,16,1,128]{3,1,2,0:T(8,128)(2,1)} %param.6), channel_id=1, source_target_pairs={{0,8},{4,12},{1,9},{5,13},{2,10},{6,14},{3,11},{7,15},{16,24},{20,... | collective-permute-start | bytes 12296 | tf_op jit(solution)/shard_map/ppermute | solution.py:13
  5.0 1.5 collective-permute-start.1
  6.5 1.0 collective-permute-done.1
  7.5 0.7 constant_dynamic-update-slice_fusion
  8.2 3.5 %collective-permute-start.2 = (bf16[3,16,1,128]{3,1,2,0:T(8,128)(2,1)S(1)}, bf16[3,16,1,128]{3,1,2,0:T(8,128)(2,1)S(1)}, u32[]{:S(2)}, u32[]{:S(2)}) collective-permute-start(bf16[3,16,1,128]{3,1,2,0:T(8,128)(2,1)S(1)} %constant_dynamic-update-slice_fusion), channel_id=1, source_target_pairs={{0,1},{1,2},{2,3},{4,5},{5,6},{6,7},{8,9},{9,10},{10,11},{12,13},{... | collective-permute-start | bytes 36872 | tf_op jit(solution)/shard_map/ppermute | solution.py:23
  11.6 1.3 collective-permute-start.3
  12.9 1.2 copy.87
  14.2 0.8 mul.79
  15.0 1.0 copy.86
  16.0 0.7 convert.1
  16.8 0.5 collective-permute-done.3
  18.2 0.6 fusion.74
  18.8 12.6 %all-reduce.5 = (f32[32]{0:T(128)S(1)}, f32[32]{0:T(128)S(1)}) all-reduce(f32[32]{0:T(128)S(1)} %get-tuple-element.6, f32[32]{0:T(128)S(1)} %get-tuple-element.5), channel_id=1, replica_groups=mesh['group'=2,'tm'=4,'space'=4] {'space'}, use_global_device_ids=true, to_apply=%region_3.4 | all-reduce | flops 64 | bytes 512 | tf_op jit(solution)/shard_map/psum | solution.py:58
  31.6 0.4 convolution_convert_fusion
  32.0 0.7 fusion.77
  32.8 14.8 %all_gather.21 = bf16[512,512]{1,0:T(8,128)(2,1)S(1)} all-gather(bf16[128,512]{1,0:T(8,128)(2,1)S(1)} %get-tuple-element.18), channel_id=1, replica_groups=mesh['group'=2,'tm'=4,'space'=4] {'space'}, dimensions={0}, use_global_device_ids=true | all-gather | bytes 655360 | tf_op jit(solution)/shard_map/all_gather | solution.py:88
  47.6 0.4 fusion.78
  48.0 0.2 exponential_reduce_fusion
  48.2 15.7 %all_gather.22 = bf16[512,512]{1,0:T(8,128)(2,1)S(1)} all-gather(bf16[128,512]{1,0:T(8,128)(2,1)S(1)} %get-tuple-element.17), channel_id=1, replica_groups=mesh['group'=2,'tm'=4,'space'=4] {'space'}, dimensions={0}, use_global_device_ids=true | all-gather | bytes 655360 | tf_op jit(solution)/shard_map/all_gather | solution.py:89
  63.9 0.3 convolution_convert_fusion.4
  64.2 0.9 multiply_reduce_fusion.2
  65.1 14.7 %all_gather.25 = bf16[512,512]{1,0:T(8,128)(2,1)S(1)} all-gather(bf16[128,512]{1,0:T(8,128)(2,1)S(1)} %get-tuple-element.26), channel_id=1, replica_groups=mesh['group'=2,'tm'=4,'space'=4] {'space'}, dimensions={0}, use_global_device_ids=true | all-gather | bytes 655360 | tf_op jit(solution)/shard_map/all_gather | solution.py:100
  79.8 1.8 %convolution_convert_fusion.3 = bf16[128,512]{1,0:T(8,128)(2,1)} fusion(bf16[512,512]{1,0:T(8,128)(2,1)S(1)} %all_gather.21, bf16[128,512]{1,0:T(8,128)(2,1)S(1)} %get-tuple-element.26, bf16[512,512]{1,0:T(8,128)(2,1)S(1)} %all_gather.22, f32[128,512]{1,0:T(8,128)S(1)} %get-tuple-element.24, f32[128]{0:T(128)} %get-tuple-element.25, f32[128]{0:T(128)} %copy-done.11), kind=kOutput, calls=%fused_computation.17 | convolution fusion | flops 134610944 | bytes 1573888 | tf_op jit(solution)/shard_map/dot_general | solution.py:94
  81.6 9.7 %all-gather = f32[4,1,128]{2,1,0:T(1,128)S(1)} all-gather(f32[1,1,128]{2,1,0:T(1,128)} %bitcast.260), channel_id=1, replica_groups=mesh['group'=2,'tm'=4,'space'=4] {'space'}, dimensions={0}, use_global_device_ids=true | all-gather | bytes 2560 | tf_op jit(solution)/shard_map/all_gather | solution.py:96
  91.3 14.9 %all_gather.23 = bf16[512,512]{1,0:T(8,128)(2,1)S(1)} all-gather(bf16[128,512]{1,0:T(8,128)(2,1)} %get-tuple-element.19), channel_id=1, replica_groups=mesh['group'=2,'tm'=4,'space'=4] {'space'}, dimensions={0}, use_global_device_ids=true | all-gather | bytes 655360 | tf_op jit(solution)/shard_map/all_gather | solution.py:99
  106.2 8.0 %all-gather.1 = f32[4,1,128]{2,1,0:T(1,128)S(1)} all-gather(f32[1,1,128]{2,1,0:T(1,128)} %bitcast.261), channel_id=1, replica_groups=mesh['group'=2,'tm'=4,'space'=4] {'space'}, dimensions={0}, use_global_device_ids=true | all-gather | bytes 2560 | tf_op jit(solution)/shard_map/all_gather | solution.py:97
  114.2 1.2 fusion.2
  115.5 0.2 convolution_convert_fusion.1
  115.7 1.5 convolution_convert_fusion.2
  117.3 0.7 multiply_reduce_fusion.1
  118.2 0.2 multiply_reduce_fusion
  118.7 10.0 %all-reduce.4 = (f32[32]{0:T(128)S(1)}, f32[32]{0:T(128)S(1)}) all-reduce(f32[32]{0:T(128)S(1)} %multiply_reduce_fusion, f32[32]{0:T(128)S(1)} %reduce_sum.67), channel_id=1, replica_groups=mesh['group'=2,'tm'=4,'space'=4] {'space'}, use_global_device_ids=true, to_apply=%region_11.12 | all-reduce | flops 64 | bytes 512 | tf_op jit(solution)/shard_map/psum | solution.py:113
  128.7 0.2 fusion.16
  129.0 1.3 collective-permute-start.4
  130.3 1.3 collective-permute-start.5
  131.6 0.6 collective-permute-done.4
  132.3 6.2 %collective-permute-done.5 = bf16[1,1,128,512]{2,3,1,0:T(8,128)(2,1)S(1)} collective-permute-done((bf16[1,1,128,512]{2,3,1,0:T(8,128)(2,1)S(1)}, bf16[1,1,128,512]{2,3,1,0:T(8,128)(2,1)S(1)}, u32[]{:S(2)}, u32[]{:S(2)}) %collective-permute-start.5) | collective-permute-done | bytes 131104 | tf_op jit(solution)/shard_map/ppermute | solution.py:13
  138.5 3.0 %collective-permute-start.6 = (bf16[3,1,128,512]{2,3,1,0:T(8,128)(2,1)S(1)}, bf16[3,1,128,512]{2,3,1,0:T(8,128)(2,1)S(1)}, u32[]{:S(2)}, u32[]{:S(2)}) collective-permute-start(bf16[3,1,128,512]{2,3,1,0:T(8,128)(2,1)S(1)} %pad_maximum_fusion.1), channel_id=1, source_target_pairs={{0,1},{1,2},{2,3},{4,5},{5,6},{6,7},{8,9},{9,10},{10,11},{12,13},{... | collective-permute-start | bytes 1179656 | tf_op jit(solution)/shard_map/ppermute | solution.py:23
  141.5 1.3 collective-permute-start.7
  142.8 0.7 fusion.76
  143.5 6.3 %collective-permute-done.6 = bf16[3,1,128,512]{2,3,1,0:T(8,128)(2,1)S(1)} collective-permute-done((bf16[3,1,128,512]{2,3,1,0:T(8,128)(2,1)S(1)}, bf16[3,1,128,512]{2,3,1,0:T(8,128)(2,1)S(1)}, u32[]{:S(2)}, u32[]{:S(2)}) %collective-permute-start.6) | collective-permute-done | bytes 393248 | tf_op jit(solution)/shard_map/ppermute | solution.py:23
  149.8 4.1 %collective-permute-done.7 = bf16[3,1,128,512]{2,3,1,0:T(8,128)(2,1)S(1)} collective-permute-done((bf16[3,1,128,512]{2,3,1,0:T(8,128)(2,1)S(1)}, bf16[3,1,128,512]{2,3,1,0:T(8,128)(2,1)S(1)}, u32[]{:S(2)}, u32[]{:S(2)}) %collective-permute-start.7) | collective-permute-done | bytes 393248 | tf_op jit(solution)/shard_map/ppermute | solution.py:24
  154.2 0.2 copy.100
  154.4 1.2 convolution_bitcast_fusion.1
  155.7 0.2 copy.105
  155.9 0.3 convolution_bitcast_fusion
  156.6 0.3 convolution_bitcast_fusion.2
  157.0 0.7 fusion.63
  (79 shorter events, 2.6 us)
Async XLA Ops:
  0.0 31.6 %copy-start = (bf16[512,1536]{1,0:T(8,128)(2,1)S(1)}, bf16[512,1536]{1,0:T(8,128)(2,1)}, u32[]{:S(2)}) copy-start(bf16[512,1536]{1,0:T(8,128)(2,1)} %param.9) | copy-start | bytes 4718596
  0.0 17.4 %copy-start.10 = (bf16[1,16,1,128]{3,1,2,0:T(8,128)(2,1)S(1)}, bf16[1,16,1,128]{3,1,2,0:T(8,128)(2,1)}, u32[]{:S(2)}) copy-start(bf16[1,16,1,128]{3,1,2,0:T(8,128)(2,1)} %param.6) | copy-start | bytes 12292
  0.0 6.5 %collective-permute-start = (bf16[1,16,1,128]{3,1,2,0:T(8,128)(2,1)}, bf16[1,16,1,128]{3,1,2,0:T(8,128)(2,1)S(1)}, u32[]{:S(2)}, u32[]{:S(2)}) collective-permute-start(bf16[1,16,1,128]{3,1,2,0:T(8,128)(2,1)} %param.6), channel_id=1, source_target_pairs={{0,8},{4,12},{1,9},{5,13},{2,10},{6,14},{3,11},{7,15},{16,24},{20,... | collective-permute-start | bytes 12296 | tf_op jit(solution)/shard_map/ppermute | solution.py:13
  5.0 2.5 %collective-permute-start.1 = (bf16[1,16,1,128]{3,1,2,0:T(8,128)(2,1)}, bf16[1,16,1,128]{3,1,2,0:T(8,128)(2,1)S(1)}, u32[]{:S(2)}, u32[]{:S(2)}) collective-permute-start(bf16[1,16,1,128]{3,1,2,0:T(8,128)(2,1)} %param.6), channel_id=1, source_target_pairs={{0,4},{4,8},{8,12},{1,5},{5,9},{9,13},{2,6},{6,10},{10,14},{3,7},{... | collective-permute-start | bytes 12296 | tf_op jit(solution)/shard_map/ppermute | solution.py:13
  8.2 8.6 %collective-permute-start.2 = (bf16[3,16,1,128]{3,1,2,0:T(8,128)(2,1)S(1)}, bf16[3,16,1,128]{3,1,2,0:T(8,128)(2,1)S(1)}, u32[]{:S(2)}, u32[]{:S(2)}) collective-permute-start(bf16[3,16,1,128]{3,1,2,0:T(8,128)(2,1)S(1)} %constant_dynamic-update-slice_fusion), channel_id=1, source_target_pairs={{0,1},{1,2},{2,3},{4,5},{5,6},{6,7},{8,9},{9,10},{10,11},{12,13},{... | collective-permute-start | bytes 36872 | tf_op jit(solution)/shard_map/ppermute | solution.py:23
  11.6 5.6 %collective-permute-start.3 = (bf16[3,16,1,128]{3,1,2,0:T(8,128)(2,1)S(1)}, bf16[3,16,1,128]{3,1,2,0:T(8,128)(2,1)S(1)}, u32[]{:S(2)}, u32[]{:S(2)}) collective-permute-start(bf16[3,16,1,128]{3,1,2,0:T(8,128)(2,1)S(1)} %constant_dynamic-update-slice_fusion), channel_id=1, source_target_pairs={{1,0},{2,1},{3,2},{5,4},{6,5},{7,6},{9,8},{10,9},{11,10},{13,12},{... | collective-permute-start | bytes 36872 | tf_op jit(solution)/shard_map/ppermute | solution.py:24
  18.8 13.2 %copy-start.2 = (f32[128,32,16]{0,1,2:T(8,128)}, f32[128,32,16]{0,1,2:T(8,128)S(1)}, u32[]{:S(2)}) copy-start(f32[128,32,16]{0,1,2:T(8,128)S(1)} %get-tuple-element.22) | copy-start | bytes 786436
  32.0 15.9 %copy-start.1 = (bf16[128,1536]{1,0:T(8,128)(2,1)}, bf16[128,1536]{1,0:T(8,128)(2,1)S(1)}, u32[]{:S(2)}) copy-start(bf16[128,1536]{1,0:T(8,128)(2,1)S(1)} %convolution_convert_fusion) | copy-start | bytes 1179652
  47.6 16.6 %copy-start.7 = (bf16[1,1,128,512]{3,2,1,0:T(8,128)(2,1)S(1)}, bf16[1,1,128,512]{3,2,1,0:T(8,128)(2,1)}, u32[]{:S(2)}) copy-start(bf16[1,1,128,512]{3,2,1,0:T(8,128)(2,1)} %param.11) | copy-start | bytes 393220
  47.6 16.7 %copy-start.8 = (bf16[512,512]{1,0:T(8,128)(2,1)S(1)}, bf16[512,512]{1,0:T(8,128)(2,1)}, u32[]{:S(2)}) copy-start(bf16[512,512]{1,0:T(8,128)(2,1)} %param.10) | copy-start | bytes 1572868
  48.2 15.8 %copy-start.11 = (f32[128]{0:T(128)}, f32[128]{0:T(128)S(1)}, u32[]{:S(2)}) copy-start(f32[128]{0:T(128)S(1)} %log_add_fusion) | copy-start | bytes 1540
  115.4 1.8 %copy-start.9 = (bf16[128,512]{1,0:T(8,128)(2,1)S(1)}, bf16[128,512]{1,0:T(8,128)(2,1)}, u32[]{:S(2)}) copy-start(bf16[128,512]{1,0:T(8,128)(2,1)} %convolution_convert_fusion.3) | copy-start | bytes 393220
  115.4 1.8 %copy-start.12 = (f32[512]{0:T(512)S(1)}, f32[512]{0:T(512)}, u32[]{:S(2)}) copy-start(f32[512]{0:T(512)} %param.8) | copy-start | bytes 6148
  117.3 1.0 copy-start.3
  117.9 10.8 %copy-start.5 = (f32[128,32,16]{0,2,1:T(8,128)S(1)}, f32[128,32,16]{0,2,1:T(8,128)}, u32[]{:S(2)}) copy-start(f32[128,32,16]{0,2,1:T(8,128)} %convert.1) | copy-start | bytes 786436
  118.2 24.6 %copy-start.4 = (bf16[3,3,3,16,512]{4,3,2,1,0:T(8,128)(2,1)S(1)}, bf16[3,3,3,16,512]{4,3,2,1,0:T(8,128)(2,1)}, u32[]{:S(2)}) copy-start(bf16[3,3,3,16,512]{4,3,2,1,0:T(8,128)(2,1)} %param.7) | copy-start | bytes 1327108
  129.0 3.2 %collective-permute-start.4 = (bf16[1,1,128,512]{2,3,1,0:T(8,128)(2,1)S(1)}, bf16[1,1,128,512]{2,3,1,0:T(8,128)(2,1)S(1)}, u32[]{:S(2)}, u32[]{:S(2)}) collective-permute-start(bf16[1,1,128,512]{2,3,1,0:T(8,128)(2,1)S(1)} %bitcast.248), channel_id=1, source_target_pairs={{4,0},{8,4},{12,8},{5,1},{9,5},{13,9},{6,2},{10,6},{14,10},{7,3},{... | collective-permute-start | bytes 393224 | tf_op jit(solution)/shard_map/ppermute | solution.py:13
  130.3 8.1 %collective-permute-start.5 = (bf16[1,1,128,512]{2,3,1,0:T(8,128)(2,1)S(1)}, bf16[1,1,128,512]{2,3,1,0:T(8,128)(2,1)S(1)}, u32[]{:S(2)}, u32[]{:S(2)}) collective-permute-start(bf16[1,1,128,512]{2,3,1,0:T(8,128)(2,1)S(1)} %bitcast.249), channel_id=1, source_target_pairs={{8,0},{12,4},{9,1},{13,5},{10,2},{14,6},{11,3},{15,7},{24,16},{28,... | collective-permute-start | bytes 393224 | tf_op jit(solution)/shard_map/ppermute | solution.py:13
  138.5 11.3 %collective-permute-start.6 = (bf16[3,1,128,512]{2,3,1,0:T(8,128)(2,1)S(1)}, bf16[3,1,128,512]{2,3,1,0:T(8,128)(2,1)S(1)}, u32[]{:S(2)}, u32[]{:S(2)}) collective-permute-start(bf16[3,1,128,512]{2,3,1,0:T(8,128)(2,1)S(1)} %pad_maximum_fusion.1), channel_id=1, source_target_pairs={{0,1},{1,2},{2,3},{4,5},{5,6},{6,7},{8,9},{9,10},{10,11},{12,13},{... | collective-permute-start | bytes 1179656 | tf_op jit(solution)/shard_map/ppermute | solution.py:23
  141.5 12.5 %collective-permute-start.7 = (bf16[3,1,128,512]{2,3,1,0:T(8,128)(2,1)S(1)}, bf16[3,1,128,512]{2,3,1,0:T(8,128)(2,1)S(1)}, u32[]{:S(2)}, u32[]{:S(2)}) collective-permute-start(bf16[3,1,128,512]{2,3,1,0:T(8,128)(2,1)S(1)} %pad_maximum_fusion.1), channel_id=1, source_target_pairs={{1,0},{2,1},{3,2},{5,4},{6,5},{7,6},{9,8},{10,9},{11,10},{13,12},{... | collective-permute-start | bytes 1179656 | tf_op jit(solution)/shard_map/ppermute | solution.py:24
  154.4 1.6 copy-start.6
where the time goes:
time: 158 us
  blocking collectives  100 us (63%)
  waiting for transfers between devices  18.7 us (12%)
  starting transfers between devices  18.1 us (11%)
  matrix products  9.75 us (6%)
  local copies, waits for them, and re-layouts  7.57 us (5%)
  other arithmetic  2.69 us (2%)
    all_gather x1, blocking collectives, on_device(): value_piece = lax.all_gather(value_part, 'space', axis=0, tiled=True)  15.7 us
    all_gather x1, blocking collectives, on_device(): query_piece = lax.all_gather(query_part, 'space', axis=0, tiled=True)  14.9 us
    all_gather x1, blocking collectives, on_device(): key_piece = lax.all_gather(key_part, 'space', axis=0, tiled=True)  14.8 us
    all_gather x1, blocking collectives, on_device(): grad_piece = lax.all_gather(grad_att, 'space', axis=0, tiled=True)  14.7 us
    psum x1, blocking collectives, on_device(): lax.psum((jnp.sum(grouped, axis=(0, 2)), jnp.sum(grouped * grouped, axis=...  12.6 us
    psum x1, blocking collectives, on_device(): lax.psum((jnp.sum(scaled, axis=(0, 2)), jnp.sum(scaled * unit_cells, axis...  10 us
    all_gather x1, blocking collectives, on_device(): lax.all_gather(log_norm, 'space', axis=0, tiled=True)  9.7 us
    ppermute x4, starting transfers between devices, from_behind(): lax.ppermute(value, axis, [(source, source + steps) for source in range(l...  9.01 us
  transfers between devices with their start and end apart: 8, of which 7 were waited for; matrix products, arithmetic and copies ran while one was open for 3% of the time, Pallas kernels for 0%

commit v1 on v0

--- a/solution.py
+++ b/solution.py
@@ -85,8 +85,13 @@
     attended = jnp.dot(soft_bf, value_piece, preferred_element_type=jnp.float32)
     attended = lax.optimization_barrier(attended.astype(jnp.bfloat16))
     row_delta = jnp.sum(grad_att.astype(jnp.float32) * attended.astype(jnp.float32), axis=1)
-    key_piece = lax.all_gather(key_part, "space", axis=0, tiled=True)
-    value_piece = lax.all_gather(value_part, "space", axis=0, tiled=True)
+    key_piece, value_piece = jnp.split(
+        lax.all_gather(
+            jnp.concatenate([key_part, value_part], axis=1), "space", axis=0, tiled=True
+        ),
+        [key_part.shape[1]],
+        axis=1,
+    )
     scores = contract(query_part, key_piece, 1, 1) * scaling
     soft_probs = jnp.exp(scores - log_norm[:, None])
     grad_probs = contract(grad_att, value_piece, 1, 1)

time: 158 us -> 174 us (1.10)
  between operations: 0.46 us -> 13.8 us
  waiting for transfers between devices: 18.7 us -> 14 us
  blocking collectives: 100 us -> 103 us
  starting transfers between devices: 18.1 us -> 20.7 us
  matrix products: 9.75 us -> 11.8 us
    all_gather x1, blocking collectives: 14.7 us -> 20.1 us  [on_device(): grad_piece = lax.all_gather(grad_att, 'space', axis=0, tiled=True)]
    ppermute x2, waiting for transfers between devices: 6.28 us -> 1.78 us  [padded_2(): before = lax.ppermute(last, axis, up)]
    ppermute x2, starting transfers between devices: 6.48 us -> 9.12 us  [padded_2(): before = lax.ppermute(last, axis, up)]
    ppermute x4, waiting for transfers between devices: 7.82 us -> 5.69 us  [from_behind(): lax.ppermute(value, axis, [(source, source + steps) for source in range(l...]
    dot_general x10 -> x11, matrix products: 7.29 us -> 9.38 us  [contract(): lax.dot_general(left, right, (((left_dim,), (right_dim,)), ((), ())), pre...]
    ppermute x2, waiting for transfers between devices: 4.6 us -> 6.51 us  [padded_2(): after = lax.ppermute(leading, axis, down)]
  transfers between devices with their start and end apart: 8 -> 9, of which waited for: 7 -> 5; matrix products, arithmetic and copies ran while one was open for 3% -> 5% of each run, Pallas kernels for 0% -> 0%
where the time goes in v1:
time: 174 us; the launch traced here: 173 us
  blocking collectives  103 us (59%)
  starting transfers between devices  20.7 us (12%)
  waiting for transfers between devices  14 us (8%)
  between operations  13.8 us (8%)
  matrix products  11.8 us (7%)
  local copies, waits for them, and re-layouts  6.76 us (4%)
  other arithmetic  2.7 us (2%)
    all_gather x1, blocking collectives, on_device(): grad_piece = lax.all_gather(grad_att, 'space', axis=0, tiled=True)  20.1 us
    all_gather x1, blocking collectives, on_device(): lax.all_gather(key_part, 'space', axis=0, tiled=True)  15.6 us
    all_gather x1, blocking collectives, on_device(): value_piece = lax.all_gather(value_part, 'space', axis=0, tiled=True)  14.8 us
    all_gather x1, blocking collectives, on_device(): query_piece = lax.all_gather(query_part, 'space', axis=0, tiled=True)  14.7 us
    psum x1, blocking collectives, on_device(): lax.psum((jnp.sum(grouped, axis=(0, 2)), jnp.sum(grouped * grouped, axis=...  10.9 us
    psum x1, blocking collectives, on_device(): lax.psum((jnp.sum(scaled, axis=(0, 2)), jnp.sum(scaled * unit_cells, axis...  9.7 us
    dot_general x11, matrix products, contract(): lax.dot_general(left, right, (((left_dim,), (right_dim,)), ((), ())), pre...  9.38 us
    ppermute x2, starting transfers between devices, padded_2(): before = lax.ppermute(last, axis, up)  9.12 us
  transfers between devices with their start and end apart: 9, of which 5 were waited for; matrix products, arithmetic and copies ran while one was open for 5% of the time, Pallas kernels for 0%

profile of v1, /device:TPU:0, one launch (start us, length us, event | category | flops | bytes accessed | tf_op | source)
XLA Modules:
  0.0 172.9 jit_solution(7407725276289976976)
XLA Ops:
  6.5 5.0 %collective-permute-start = (bf16[1,16,1,128]{3,1,2,0:T(8,128)(2,1)}, bf16[1,16,1,128]{3,1,2,0:T(8,128)(2,1)S(1)}, u32[]{:S(2)}, u32[]{:S(2)}) collective-permute-start(bf16[1,16,1,128]{3,1,2,0:T(8,128)(2,1)} %param.6), channel_id=1, source_target_pairs={{0,8},{4,12},{1,9},{5,13},{2,10},{6,14},{3,11},{7,15},{16,24},{20,... | collective-permute-start | bytes 12296 | tf_op jit(solution)/shard_map/ppermute | solution.py:13
  11.5 1.5 collective-permute-start.1
  13.1 1.0 collective-permute-done.1
  14.0 0.7 constant_dynamic-update-slice_fusion
  14.7 1.3 collective-permute-start.3
  16.0 4.5 %collective-permute-start.2 = (bf16[3,16,1,128]{3,1,2,0:T(8,128)(2,1)S(1)}, bf16[3,16,1,128]{3,1,2,0:T(8,128)(2,1)S(1)}, u32[]{:S(2)}, u32[]{:S(2)}) collective-permute-start(bf16[3,16,1,128]{3,1,2,0:T(8,128)(2,1)S(1)} %constant_dynamic-update-slice_fusion), channel_id=1, source_target_pairs={{0,1},{1,2},{2,3},{4,5},{5,6},{6,7},{8,9},{9,10},{10,11},{12,13},{... | collective-permute-start | bytes 36872 | tf_op jit(solution)/shard_map/ppermute | solution.py:23
  20.6 1.0 copy.86
  21.6 0.7 convert.1
  22.3 1.2 copy.87
  24.7 0.5 fusion.78
  25.2 10.9 %all-reduce.5 = (f32[32]{0:T(128)S(1)}, f32[32]{0:T(128)S(1)}) all-reduce(f32[32]{0:T(128)S(1)} %get-tuple-element.6, f32[32]{0:T(128)S(1)} %get-tuple-element.5), channel_id=1, replica_groups=mesh['group'=2,'tm'=4,'space'=4] {'space'}, use_global_device_ids=true, to_apply=%region_3.4 | all-reduce | flops 64 | bytes 512 | tf_op jit(solution)/shard_map/psum | solution.py:58
  36.2 0.1 multiply_convert_fusion
  36.4 0.4 convolution_convert_fusion
  36.8 0.7 concatenate.28
  37.6 14.8 %all_gather.24 = bf16[512,512]{1,0:T(8,128)(2,1)S(1)} all-gather(bf16[128,512]{1,0:T(8,128)(2,1)S(1)} %get-tuple-element.17), channel_id=1, replica_groups=mesh['group'=2,'tm'=4,'space'=4] {'space'}, dimensions={0}, use_global_device_ids=true | all-gather | bytes 655360 | tf_op jit(solution)/shard_map/all_gather | solution.py:82
  52.4 15.6 %all_gather.23 = bf16[512,512]{1,0:T(8,128)(2,1)S(1)} all-gather(bf16[128,512]{1,0:T(8,128)(2,1)S(1)} %get-tuple-element.18), channel_id=1, replica_groups=mesh['group'=2,'tm'=4,'space'=4] {'space'}, dimensions={0}, use_global_device_ids=true | all-gather | bytes 655360 | tf_op jit(solution)/shard_map/all_gather | solution.py:75
  67.9 0.4 fusion.82
  68.3 0.2 exponential_reduce_fusion
  68.6 0.3 convolution_convert_fusion.4
  68.8 8.9 %all-gather = f32[4,1,128]{2,1,0:T(1,128)S(1)} all-gather(f32[1,1,128]{2,1,0:T(1,128)S(1)} %bitcast.258), channel_id=1, replica_groups=mesh['group'=2,'tm'=4,'space'=4] {'space'}, dimensions={0}, use_global_device_ids=true | all-gather | bytes 2560 | tf_op jit(solution)/shard_map/all_gather | solution.py:101
  77.8 1.4 multiply_reduce_fusion.2
  79.2 8.4 %all-gather.1 = f32[4,1,128]{2,1,0:T(1,128)} all-gather(f32[1,1,128]{2,1,0:T(1,128)S(1)} %bitcast.259), channel_id=1, replica_groups=mesh['group'=2,'tm'=4,'space'=4] {'space'}, dimensions={0}, use_global_device_ids=true | all-gather | bytes 2560 | tf_op jit(solution)/shard_map/all_gather | solution.py:102
  87.6 20.1 %all_gather.27 = bf16[512,512]{1,0:T(8,128)(2,1)S(1)} all-gather(bf16[128,512]{1,0:T(8,128)(2,1)S(1)} %get-tuple-element.26), channel_id=1, replica_groups=mesh['group'=2,'tm'=4,'space'=4] {'space'}, dimensions={0}, use_global_device_ids=true | all-gather | bytes 655360 | tf_op jit(solution)/shard_map/all_gather | solution.py:105
  107.7 14.7 %all_gather.25 = bf16[512,512]{1,0:T(8,128)(2,1)S(1)} all-gather(bf16[128,512]{1,0:T(8,128)(2,1)S(1)} %get-tuple-element.19), channel_id=1, replica_groups=mesh['group'=2,'tm'=4,'space'=4] {'space'}, dimensions={0}, use_global_device_ids=true | all-gather | bytes 655360 | tf_op jit(solution)/shard_map/all_gather | solution.py:104
  122.4 0.3 fusion.4
  122.7 0.9 convolution_convert_fusion.1
  123.6 2.0 %convolution_convert_fusion.2 = bf16[128,512]{1,0:T(8,128)(2,1)} fusion(bf16[512,512]{1,0:T(8,128)(2,1)S(1)} %all_gather.25, f32[512,128]{1,0:T(8,128)S(1)} %fusion.4, bf16[512,512]{1,0:T(8,128)(2,1)S(1)} %all_gather.27, f32[512]{0:T(512)} %bitcast.257, bf16[128,1536]{1,0:T(8,128)(2,1)S(1)} %convolution_convert_fusion), kind=kOutput, calls=%fused_computation.19 | convolution fusion | flops 134545408 | bytes 1574912 | tf_op jit(solution)/shard_map/dot_general | solution.py:30
  125.6 1.4 fusion.1
  127.0 1.7 convolution_convert_fusion.3
  128.8 0.6 multiply_reduce_fusion.1
  129.6 0.2 multiply_reduce_fusion
  130.0 9.7 %all-reduce.4 = (f32[32]{0:T(128)S(1)}, f32[32]{0:T(128)S(1)}) all-reduce(f32[32]{0:T(128)S(1)} %multiply_reduce_fusion, f32[32]{0:T(128)S(1)} %reduce_sum.67), channel_id=1, replica_groups=mesh['group'=2,'tm'=4,'space'=4] {'space'}, use_global_device_ids=true, to_apply=%region_11.12 | all-reduce | flops 64 | bytes 512 | tf_op jit(solution)/shard_map/psum | solution.py:118
  139.7 0.2 fusion.22
  140.1 1.3 collective-permute-start.5
  141.4 1.3 collective-permute-start.4
  142.7 4.7 %collective-permute-done.5 = bf16[1,1,128,512]{2,3,1,0:T(8,128)(2,1)S(1)} collective-permute-done((bf16[1,1,128,512]{2,3,1,0:T(8,128)(2,1)S(1)}, bf16[1,1,128,512]{2,3,1,0:T(8,128)(2,1)S(1)}, u32[]{:S(2)}, u32[]{:S(2)}) %collective-permute-start.5) | collective-permute-done | bytes 131104 | tf_op jit(solution)/shard_map/ppermute | solution.py:13
  147.4 1.3 collective-permute-start.7
  148.7 4.6 %collective-permute-start.6 = (bf16[3,1,128,512]{2,3,1,0:T(8,128)(2,1)S(1)}, bf16[3,1,128,512]{2,3,1,0:T(8,128)(2,1)S(1)}, u32[]{:S(2)}, u32[]{:S(2)}) collective-permute-start(bf16[3,1,128,512]{2,3,1,0:T(8,128)(2,1)S(1)} %pad_maximum_fusion.1), channel_id=1, source_target_pairs={{0,1},{1,2},{2,3},{4,5},{5,6},{6,7},{8,9},{9,10},{10,11},{12,13},{... | collective-permute-start | bytes 1179656 | tf_op jit(solution)/shard_map/ppermute | solution.py:23
  153.3 0.7 fusion.80
  154.0 6.5 %collective-permute-done.7 = bf16[3,1,128,512]{2,3,1,0:T(8,128)(2,1)S(1)} collective-permute-done((bf16[3,1,128,512]{2,3,1,0:T(8,128)(2,1)S(1)}, bf16[3,1,128,512]{2,3,1,0:T(8,128)(2,1)S(1)}, u32[]{:S(2)}, u32[]{:S(2)}) %collective-permute-start.7) | collective-permute-done | bytes 393248 | tf_op jit(solution)/shard_map/ppermute | solution.py:24
  160.5 1.8 %collective-permute-done.6 = bf16[3,1,128,512]{2,3,1,0:T(8,128)(2,1)S(1)} collective-permute-done((bf16[3,1,128,512]{2,3,1,0:T(8,128)(2,1)S(1)}, bf16[3,1,128,512]{2,3,1,0:T(8,128)(2,1)S(1)}, u32[]{:S(2)}, u32[]{:S(2)}) %collective-permute-start.6) | collective-permute-done | bytes 393248 | tf_op jit(solution)/shard_map/ppermute | solution.py:23
  162.5 0.2 copy.105
  162.7 1.2 convolution_bitcast_fusion
  164.1 0.2 copy.100
  164.3 0.3 convolution_bitcast_fusion.1
  164.7 0.2 copy.95
  164.9 0.3 convolution_bitcast_fusion.2
  165.3 0.7 fusion.66
  (84 shorter events, 2.3 us)
Async XLA Ops:
  6.5 29.9 %copy-start = (bf16[512,1536]{1,0:T(8,128)(2,1)S(1)}, bf16[512,1536]{1,0:T(8,128)(2,1)}, u32[]{:S(2)}) copy-start(bf16[512,1536]{1,0:T(8,128)(2,1)} %param.9) | copy-start | bytes 4718596
  6.5 17.4 %copy-start.8 = (bf16[1,16,1,128]{3,1,2,0:T(8,128)(2,1)S(1)}, bf16[1,16,1,128]{3,1,2,0:T(8,128)(2,1)}, u32[]{:S(2)}) copy-start(bf16[1,16,1,128]{3,1,2,0:T(8,128)(2,1)} %param.6) | copy-start | bytes 12292
  6.5 17.0 %copy-start.11 = (f32[512]{0:T(512)S(1)}, f32[512]{0:T(512)}, u32[]{:S(2)}) copy-start(f32[512]{0:T(512)} %param.8) | copy-start | bytes 6148
  6.5 119.1 %all-gather.4.cloned.1.call-start = ((), (), s32[]{:S(2)}) async-start(), calls=%async_computation | async-start | bytes 1310720 | tf_op jit(solution)/shard_map/all_gather | solution.py:89
  6.5 6.5 %collective-permute-start = (bf16[1,16,1,128]{3,1,2,0:T(8,128)(2,1)}, bf16[1,16,1,128]{3,1,2,0:T(8,128)(2,1)S(1)}, u32[]{:S(2)}, u32[]{:S(2)}) collective-permute-start(bf16[1,16,1,128]{3,1,2,0:T(8,128)(2,1)} %param.6), channel_id=1, source_target_pairs={{0,8},{4,12},{1,9},{5,13},{2,10},{6,14},{3,11},{7,15},{16,24},{20,... | collective-permute-start | bytes 12296 | tf_op jit(solution)/shard_map/ppermute | solution.py:13
  11.5 2.5 %collective-permute-start.1 = (bf16[1,16,1,128]{3,1,2,0:T(8,128)(2,1)}, bf16[1,16,1,128]{3,1,2,0:T(8,128)(2,1)S(1)}, u32[]{:S(2)}, u32[]{:S(2)}) collective-permute-start(bf16[1,16,1,128]{3,1,2,0:T(8,128)(2,1)} %param.6), channel_id=1, source_target_pairs={{0,4},{4,8},{8,12},{1,5},{5,9},{9,13},{2,6},{6,10},{10,14},{3,7},{... | collective-permute-start | bytes 12296 | tf_op jit(solution)/shard_map/ppermute | solution.py:13
  14.7 9.0 %collective-permute-start.3 = (bf16[3,16,1,128]{3,1,2,0:T(8,128)(2,1)S(1)}, bf16[3,16,1,128]{3,1,2,0:T(8,128)(2,1)S(1)}, u32[]{:S(2)}, u32[]{:S(2)}) collective-permute-start(bf16[3,16,1,128]{3,1,2,0:T(8,128)(2,1)S(1)} %constant_dynamic-update-slice_fusion), channel_id=1, source_target_pairs={{1,0},{2,1},{3,2},{5,4},{6,5},{7,6},{9,8},{10,9},{11,10},{13,12},{... | collective-permute-start | bytes 36872 | tf_op jit(solution)/shard_map/ppermute | solution.py:24
  16.0 7.7 %collective-permute-start.2 = (bf16[3,16,1,128]{3,1,2,0:T(8,128)(2,1)S(1)}, bf16[3,16,1,128]{3,1,2,0:T(8,128)(2,1)S(1)}, u32[]{:S(2)}, u32[]{:S(2)}) collective-permute-start(bf16[3,16,1,128]{3,1,2,0:T(8,128)(2,1)S(1)} %constant_dynamic-update-slice_fusion), channel_id=1, source_target_pairs={{0,1},{1,2},{2,3},{4,5},{5,6},{6,7},{8,9},{9,10},{10,11},{12,13},{... | collective-permute-start | bytes 36872 | tf_op jit(solution)/shard_map/ppermute | solution.py:23
  67.9 9.8 %copy-start.5 = (bf16[1,1,128,512]{3,2,1,0:T(8,128)(2,1)S(1)}, bf16[1,1,128,512]{3,2,1,0:T(8,128)(2,1)}, u32[]{:S(2)}) copy-start(bf16[1,1,128,512]{3,2,1,0:T(8,128)(2,1)} %param.11) | copy-start | bytes 393220
  68.5 39.2 %copy-start.9 = (f32[128]{0:T(128)}, f32[128]{0:T(128)S(1)}, u32[]{:S(2)}) copy-start(f32[128]{0:T(128)S(1)} %log_add_fusion) | copy-start | bytes 1540
  79.2 28.6 %copy-start.10 = (f32[128]{0:T(128)}, f32[128]{0:T(128)S(1)}, u32[]{:S(2)}) copy-start(f32[128]{0:T(128)S(1)} %get-tuple-element.25) | copy-start | bytes 1540
  79.2 43.2 %copy-start.4 = (bf16[128,512]{1,0:T(8,128)(2,1)}, bf16[128,512]{1,0:T(8,128)(2,1)S(1)}, u32[]{:S(2)}) copy-start(bf16[128,512]{1,0:T(8,128)(2,1)S(1)} %get-tuple-element.26) | copy-start | bytes 393220
  125.6 3.2 %copy-start.6 = (bf16[128,512]{1,0:T(8,128)(2,1)S(1)}, bf16[128,512]{1,0:T(8,128)(2,1)}, u32[]{:S(2)}) copy-start(bf16[128,512]{1,0:T(8,128)(2,1)} %convolution_convert_fusion.1) | copy-start | bytes 393220
  125.6 3.2 %copy-start.7 = (bf16[128,512]{1,0:T(8,128)(2,1)S(1)}, bf16[128,512]{1,0:T(8,128)(2,1)}, u32[]{:S(2)}) copy-start(bf16[128,512]{1,0:T(8,128)(2,1)} %convolution_convert_fusion.2) | copy-start | bytes 393220
  125.6 3.2 %copy-start.12 = (f32[512]{0:T(512)S(1)}, f32[512]{0:T(512)}, u32[]{:S(2)}) copy-start(f32[512]{0:T(512)} %param.8) | copy-start | bytes 6148
  129.4 10.3 %copy-start.2 = (f32[128,32,16]{0,2,1:T(8,128)S(1)}, f32[128,32,16]{0,2,1:T(8,128)}, u32[]{:S(2)}) copy-start(f32[128,32,16]{0,2,1:T(8,128)} %convert.1) | copy-start | bytes 786436
  129.6 23.7 %copy-start.1 = (bf16[3,3,3,16,512]{4,3,2,1,0:T(8,128)(2,1)S(1)}, bf16[3,3,3,16,512]{4,3,2,1,0:T(8,128)(2,1)}, u32[]{:S(2)}) copy-start(bf16[3,3,3,16,512]{4,3,2,1,0:T(8,128)(2,1)} %param.7) | copy-start | bytes 1327108
  140.1 7.3 %collective-permute-start.5 = (bf16[1,1,128,512]{2,3,1,0:T(8,128)(2,1)S(1)}, bf16[1,1,128,512]{2,3,1,0:T(8,128)(2,1)S(1)}, u32[]{:S(2)}, u32[]{:S(2)}) collective-permute-start(bf16[1,1,128,512]{2,3,1,0:T(8,128)(2,1)S(1)} %bitcast.246), channel_id=1, source_target_pairs={{8,0},{12,4},{9,1},{13,5},{10,2},{14,6},{11,3},{15,7},{24,16},{28,... | collective-permute-start | bytes 393224 | tf_op jit(solution)/shard_map/ppermute | solution.py:13
  141.4 6.0 %collective-permute-start.4 = (bf16[1,1,128,512]{2,3,1,0:T(8,128)(2,1)S(1)}, bf16[1,1,128,512]{2,3,1,0:T(8,128)(2,1)S(1)}, u32[]{:S(2)}, u32[]{:S(2)}) collective-permute-start(bf16[1,1,128,512]{2,3,1,0:T(8,128)(2,1)S(1)} %bitcast.247), channel_id=1, source_target_pairs={{4,0},{8,4},{12,8},{5,1},{9,5},{13,9},{6,2},{10,6},{14,10},{7,3},{... | collective-permute-start | bytes 393224 | tf_op jit(solution)/shard_map/ppermute | solution.py:13
  147.4 13.1 %collective-permute-start.7 = (bf16[3,1,128,512]{2,3,1,0:T(8,128)(2,1)S(1)}, bf16[3,1,128,512]{2,3,1,0:T(8,128)(2,1)S(1)}, u32[]{:S(2)}, u32[]{:S(2)}) collective-permute-start(bf16[3,1,128,512]{2,3,1,0:T(8,128)(2,1)S(1)} %pad_maximum_fusion.1), channel_id=1, source_target_pairs={{1,0},{2,1},{3,2},{5,4},{6,5},{7,6},{9,8},{10,9},{11,10},{13,12},{... | collective-permute-start | bytes 1179656 | tf_op jit(solution)/shard_map/ppermute | solution.py:24
  148.7 13.6 %collective-permute-start.6 = (bf16[3,1,128,512]{2,3,1,0:T(8,128)(2,1)S(1)}, bf16[3,1,128,512]{2,3,1,0:T(8,128)(2,1)S(1)}, u32[]{:S(2)}, u32[]{:S(2)}) collective-permute-start(bf16[3,1,128,512]{2,3,1,0:T(8,128)(2,1)S(1)} %pad_maximum_fusion.1), channel_id=1, source_target_pairs={{0,1},{1,2},{2,3},{4,5},{5,6},{6,7},{8,9},{9,10},{10,11},{12,13},{... | collective-permute-start | bytes 1179656 | tf_op jit(solution)/shard_map/ppermute | solution.py:23
  162.7 1.6 copy-start.3
Sparse Core Ops, SparseCore 0:
  68.7 38.3 all-gather.3
